TPU v7x, 256 devices: a whole 4x4x8 slice. The times are simulated.
256 devices in a mesh: section: 16 (over z_lo, y), dp: 16 (over x, z_hi, core).
Axes of the slice: x: 4, y: 4, z: 8 (z_hi: 2, z_lo: 4; z = z_hi * 4 + z_lo), core: 2. Of those that a mesh axis runs over, the one named last changes fastest.
Arguments:
- enc_state: bfloat16 [16, 512, 4096], P('section', 'dp'), may hold values from -1000 to 1000
- final_gain: float32 [4096], replicated, may hold values from 0.5 to 1.5
- queries: bfloat16 [16, 2048, 4096], P('section', 'dp'), may hold values from -60 to 60
- w_key: bfloat16 [16, 4096, 4096], P('section', None, 'dp'), may hold values from -0.09375 to 0.09375
- w_value: bfloat16 [16, 4096, 4096], P('section', None, 'dp'), may hold values from -0.09375 to 0.09375
- ctx_grad: bfloat16 [16, 2048, 4096], P('section', 'dp'), may hold values from -6 to 6
- mem_len: int32 [16], P('dp'), may hold values from 8 to 32, as said below
Outputs:
- query_grad: bfloat16 [16, 2048, 4096], P('section', 'dp')
- key_weight_grad: bfloat16 [16, 4096, 4096], P('section', None, 'dp')
- value_weight_grad: bfloat16 [16, 4096, 4096], P('section', None, 'dp')
- state_grad: bfloat16 [16, 512, 4096], P('section', 'dp')
- gain_grad: float32 [4096], replicated
Inputs may be any that keep to these rules, and one draw needn't show every extreme that they name: Sequence b's memory holds mem_len[b] valid tokens from position 0; in every draw some sequence has all 32.
All inputs are finite; a program needn't handle non-finite values.
Results may differ from a plain program's by a relative error of at most 0.028.
The roundings to bfloat16 on the way count: a program that leaves them out, or rounds other values in their place, can miss the bound.
Values may be sent and summed in bfloat16 or wider, within the bound.
A program may use at most 64 MiB of HBM per device.

v0:
```python
import jax
import jax.numpy as jnp
from jax import lax
from jax.sharding import PartitionSpec as P

HEAD_DIM = 256
epsilon = 1e-06


def broadcast(block, axis, holder):
    block = jnp.where(lax.axis_index(axis) == holder, block, jnp.zeros_like(block))
    return lax.psum(block, axis)


def on_device(enc_state, final_gain, queries, w_key, w_value, ctx_grad, mem_len):
    sections = lax.axis_size("section")
    replicas = lax.axis_size("dp")
    section_index = lax.axis_index("section")
    last_encoder = sections // 2 - 1
    is_decoder = (section_index > last_encoder).astype(jnp.float32)
    is_last = (section_index == last_encoder).astype(jnp.float32)
    src_len = enc_state.shape[1]
    tgt_len = queries.shape[1]
    local_width = w_key.shape[2]
    heads_here = local_width // HEAD_DIM
    score_scale = HEAD_DIM ** (-0.5)
    enc_rows = enc_state[0].astype(jnp.float32)
    inverse = lax.rsqrt(jnp.mean(enc_rows * enc_rows, axis=1, keepdims=True) + epsilon)
    normed = enc_rows * inverse
    memory = (normed * final_gain).astype(jnp.bfloat16)
    sent = broadcast(memory, "section", last_encoder)
    all_memory, all_len = (
        lax.all_gather(sent, "dp", axis=0, tiled=True),
        lax.all_gather(mem_len, "dp", axis=0, tiled=True),
    )
    w_both = jnp.concatenate([w_key[0], w_value[0]], axis=1)
    projected = jnp.dot(all_memory, w_both, preferred_element_type=jnp.float32).astype(jnp.bfloat16)
    key_rows = projected[:, :local_width].reshape(replicas, src_len, heads_here, HEAD_DIM)
    value_rows = projected[:, local_width:].reshape(replicas, src_len, heads_here, HEAD_DIM)
    query_heads, grad_heads = (
        lax.all_to_all(queries[0], "dp", split_axis=1, concat_axis=0, tiled=True),
        lax.all_to_all(ctx_grad[0], "dp", split_axis=1, concat_axis=0, tiled=True),
    )
    query_rows = query_heads.reshape(replicas, tgt_len, heads_here, HEAD_DIM)
    grad_rows = grad_heads.reshape(replicas, tgt_len, heads_here, HEAD_DIM)
    key_valid = jnp.arange(src_len, dtype=jnp.int32)[None, :] < all_len[:, None]
    scores = (
        jnp.einsum("btha,buha->bhut", query_rows, key_rows, preferred_element_type=jnp.float32)
        * score_scale
    )
    scores = jnp.where(key_valid[:, None, :, None], scores, -1e30)
    row_max = jnp.max(scores, axis=2, keepdims=True)
    exponent = jnp.exp(scores - row_max)
    probs = exponent / jnp.sum(exponent, axis=2, keepdims=True)
    probs_low = probs.astype(jnp.bfloat16)
    grad_probs = jnp.einsum(
        "btha,buha->bhut", grad_rows, value_rows, preferred_element_type=jnp.float32
    )
    row_delta = jnp.sum(probs * grad_probs, axis=2, keepdims=True)
    grad_scores = (probs * (grad_probs - row_delta) * score_scale).astype(jnp.bfloat16)
    query_grad_heads = (
        jnp.einsum("bhut,buha->btha", grad_scores, key_rows, preferred_element_type=jnp.float32)
        .astype(jnp.bfloat16)
        .reshape(replicas * tgt_len, local_width)
    )
    key_grad = (
        jnp.einsum("bhut,btha->buha", grad_scores, query_rows, preferred_element_type=jnp.float32)
        .astype(jnp.bfloat16)
        .reshape(replicas * src_len, local_width)
    )
    value_grad = (
        jnp.einsum("bhut,btha->buha", probs_low, grad_rows, preferred_element_type=jnp.float32)
        .astype(jnp.bfloat16)
        .reshape(replicas * src_len, local_width)
    )
    both_grads = jnp.concatenate([key_grad, value_grad], axis=1)
    weight_grads = (
        lax.dot_general(
            all_memory, both_grads, (((0,), (0,)), ((), ())), preferred_element_type=jnp.float32
        )
        * is_decoder
    ).astype(jnp.bfloat16)
    query_back = lax.all_to_all(query_grad_heads, "dp", split_axis=0, concat_axis=1, tiled=True)
    query_grad = (query_back.astype(jnp.float32) * is_decoder).astype(jnp.bfloat16)[None]
    section_part = lax.psum_scatter(
        (
            lax.dot_general(
                both_grads, w_both, (((1,), (1,)), ((), ())), preferred_element_type=jnp.float32
            )
            * is_decoder
        ).astype(jnp.bfloat16),
        "dp",
        scatter_dimension=0,
        tiled=True,
    )
    memory_grad = lax.psum(section_part, "section").astype(jnp.float32)
    scaled_grad = memory_grad * final_gain
    last_grad = inverse * (
        scaled_grad - normed * jnp.mean(scaled_grad * normed, axis=1, keepdims=True)
    )
    state_grad = (last_grad * is_last).astype(jnp.bfloat16)[None]
    gain_grad = lax.psum(jnp.sum(memory_grad * normed, axis=0) * is_last, ("section", "dp"))
    key_weight_grad = weight_grads[:, :local_width][None]
    value_weight_grad = weight_grads[:, local_width:][None]
    return (query_grad, key_weight_grad, value_weight_grad, state_grad, gain_grad)


def solution(mesh):
    placed = (
        P("section", "dp", None),
        P(),
        P("section", "dp", None),
        P("section", None, "dp"),
        P("section", None, "dp"),
        P("section", "dp", None),
        P("dp"),
    )
    return jax.shard_map(
        on_device,
        mesh=mesh,
        in_specs=placed,
        out_specs=(
            P("section", "dp", None),
            P("section", None, "dp"),
            P("section", None, "dp"),
            P("section", "dp", None),
            P(),
        ),
        check_vma=False,
    )
```

profile of v0, /device:TPU:1, one launch (start us, length us, event | category | flops | bytes accessed | tf_op | source)
XLA Modules:
  0.0 639.9 jit_solution(12333519288310503521)
XLA Ops:
  7.2 0.0 copy-start.1
  7.2 0.0 all-reduce.4.cloned.1.call-start
  7.2 1.2 fusion.28
  8.4 1.8 fusion.33
  10.2 0.0 all-reduce.4.cloned.1.call-update
  10.3 0.0 all-gather.2.cloned.1.call-start
  10.3 156.1 %all-reduce.4.cloned.1.call-done = bf16[32,4096]{1,0:T(8,128)(2,1)} async-done(((bf16[32,4096]{1,0:T(8,128)(2,1)}), bf16[32,4096]{1,0:T(8,128)(2,1)}) %all-reduce.4.cloned.1.call-update) | async-done | bytes 262160 | tf_op jit(solution)/shard_map/psum | solution.py:12
  166.4 0.0 all-gather.2.cloned.1.call-update
  166.4 1.6 copy.13
  168.0 1.3 copy.14
  169.3 19.1 %all-to-all-start = ((bf16[128,16,256]{2,0,1:T(8,128)(2,1)}), bf16[128,16,256]{2,0,1:T(8,128)(2,1)S(1)}, u32[]{:S(2)}, u32[]{:S(2)}) async-start(bf16[128,16,256]{2,0,1:T(8,128)(2,1)} %copy.14), calls=%async_computation | async-start | bytes 2097152 | tf_op jit(solution)/shard_map/all_to_all | solution.py:41
  188.4 0.0 copy-done.1
  188.4 0.7 copy.15
  189.1 1.3 copy.16
  190.4 26.1 %all-to-all-done = bf16[128,16,256]{2,0,1:T(8,128)(2,1)S(1)} async-done(((bf16[128,16,256]{2,0,1:T(8,128)(2,1)}), bf16[128,16,256]{2,0,1:T(8,128)(2,1)S(1)}, u32[]{:S(2)}, u32[]{:S(2)}) %all-to-all-start) | async-done | bytes 1048608 | tf_op jit(solution)/shard_map/all_to_all | solution.py:41
  216.5 7.5 %all-to-all-start.1 = ((bf16[128,16,256]{2,0,1:T(8,128)(2,1)}), bf16[128,16,256]{2,0,1:T(8,128)(2,1)S(1)}, u32[]{:S(2)}, u32[]{:S(2)}) async-start(bf16[128,16,256]{2,0,1:T(8,128)(2,1)} %copy.16), calls=%async_computation.1 | async-start | bytes 2097152 | tf_op jit(solution)/shard_map/all_to_all | solution.py:42
  224.0 0.0 reduce-scatter.2.cloned.1.call-start
  224.7 0.0 copy-done.3
  224.7 0.6 dynamic-slice
  225.3 0.8 dynamic-update-slice
  226.0 33.3 %all-reduce = s32[16]{0:T(128)S(1)} all-reduce(s32[16]{0:T(128)S(1)} %dynamic-update-slice), channel_id=1, replica_groups=mesh['section'=16,'dp'=16] {'dp'}, use_global_device_ids=true, to_apply=%add | all-reduce | flops 16 | bytes 128
  259.3 0.1 iota_compare_fusion
  259.4 15.6 %all-gather.2.cloned.1.call-done = bf16[512,4096]{1,0:T(8,128)(2,1)} async-done(((bf16[32,4096]{1,0:T(8,128)(2,1)}), bf16[512,4096]{1,0:T(8,128)(2,1)}) %all-gather.2.cloned.1.call-update) | async-done | bytes 4194320 | tf_op jit(solution)/shard_map/all_gather | solution.py:33
  275.0 5.8 fusion.4
  280.8 0.5 fusion.10
  281.3 0.6 fusion.46
  281.9 0.0 all-to-all-done.1
  281.9 0.5 fusion.13
  282.4 0.3 convolution_convert_fusion.1
  282.7 0.3 convolution_convert_fusion.2
  283.0 6.6 %multiply_convert_fusion = bf16[512,4096]{1,0:T(8,128)(2,1)} fusion(f32[]{:T(128)S(6)} %convert_element_type.108, bf16[4096,256]{1,0:T(8,128)(2,1)} %bitcast.67, bf16[4096,256]{1,0:T(8,128)(2,1)} %bitcast.69, bf16[512,256]{1,0:T(8,128)(2,1)S(1)} %bitcast.70, bf16[512,256]{1,0:T(8,128)(2,1)S(1)} %bitcast.72), kind=kOutput, calls=%fused_computation.2 | convolution fusion | flops 2161115136 | bytes 8912900 | tf_op jit(solution)/shard_map/dot_general | solution.py:87
  289.6 0.0 reduce-scatter.2.cloned.1.call-update
  289.6 1.5 fusion.3
  291.1 3.7 all-to-all-start.2
  294.8 0.0 all-reduce.6.cloned.1.call-start
  294.8 4.6 multiply_convert_fusion.1
  299.4 2.3 slice_bitcast_fusion
  301.7 91.4 %reduce-scatter.2.cloned.1.call-done = bf16[32,4096]{1,0:T(8,128)(2,1)} async-done(((bf16[512,4096]{1,0:T(8,128)(2,1)}), bf16[32,4096]{1,0:T(8,128)(2,1)}) %reduce-scatter.2.cloned.1.call-update) | async-done | bytes 262160 | tf_op jit(solution)/shard_map/reduce_scatter | solution.py:85
  393.1 0.0 all-reduce.6.cloned.1.call-update
  393.2 0.0 all-to-all-done.2
  393.2 0.3 multiply_convert_fusion.2
  393.5 1.3 copy.17
  394.8 150.1 %all-reduce.6.cloned.1.call-done = bf16[32,4096]{1,0:T(8,128)(2,1)} async-done(((bf16[32,4096]{1,0:T(8,128)(2,1)}), bf16[32,4096]{1,0:T(8,128)(2,1)}) %all-reduce.6.cloned.1.call-update) | async-done | bytes 262160 | tf_op jit(solution)/shard_map/psum | solution.py:96
  544.9 0.0 copy-done
  544.9 0.0 copy-done.2
  544.9 1.3 fusion.27
  546.2 85.3 %psum.23 = f32[4096]{0:T(1024)} all-reduce(f32[4096]{0:T(1024)S(1)} %broadcast_multiply_fusion), channel_id=1, replica_groups=mesh['section'=16,'dp'=16] {'section','dp'}, use_global_device_ids=true, to_apply=%region_9.10 | all-reduce | flops 4096 | bytes 32768 | tf_op jit(solution)/shard_map/psum | solution.py:102
  631.5 1.8 fusion.34
  (8 shorter events, 0.1 us)
Async XLA Ops:
  7.2 181.2 %copy-start.1 = (bf16[1,128,4096]{2,1,0:T(8,128)(2,1)S(1)}, bf16[1,128,4096]{2,1,0:T(8,128)(2,1)}, u32[]{:S(2)}) copy-start(bf16[1,128,4096]{2,1,0:T(8,128)(2,1)} %param.12) | copy-start | bytes 3145732
  7.2 159.2 %all-reduce.4.cloned.1.call-start = ((), (), s32[]{:S(2)}) async-start(), calls=%async_computation.4 | async-start | bytes 524288 | tf_op jit(solution)/shard_map/psum | solution.py:12
  10.3 264.7 %all-gather.2.cloned.1.call-start = ((), (), s32[]{:S(2)}) async-start(), calls=%async_computation.5 | async-start | bytes 4456448 | tf_op jit(solution)/shard_map/all_gather | solution.py:33
  169.3 55.3 %copy-start.3 = (u32[256]{0:T(256)S(1)}, u32[256]{0:T(256)}, u32[]{:S(2)}) copy-start(u32[256]{0:T(256)} %constant.31) | copy-start | bytes 3076
  169.3 47.2 %all-to-all-start = ((bf16[128,16,256]{2,0,1:T(8,128)(2,1)}), bf16[128,16,256]{2,0,1:T(8,128)(2,1)S(1)}, u32[]{:S(2)}, u32[]{:S(2)}) async-start(bf16[128,16,256]{2,0,1:T(8,128)(2,1)} %copy.14), calls=%async_computation | async-start | bytes 2097152 | tf_op jit(solution)/shard_map/all_to_all | solution.py:41
  216.5 65.4 %all-to-all-start.1 = ((bf16[128,16,256]{2,0,1:T(8,128)(2,1)}), bf16[128,16,256]{2,0,1:T(8,128)(2,1)S(1)}, u32[]{:S(2)}, u32[]{:S(2)}) async-start(bf16[128,16,256]{2,0,1:T(8,128)(2,1)} %copy.16), calls=%async_computation.1 | async-start | bytes 2097152 | tf_op jit(solution)/shard_map/all_to_all | solution.py:42
  224.0 169.2 %reduce-scatter.2.cloned.1.call-start = ((), (), s32[]{:S(2)}) async-start(), calls=%async_computation.6 | async-start | bytes 4456448 | tf_op jit(solution)/shard_map/reduce_scatter | solution.py:85
  291.1 102.1 %all-to-all-start.2 = ((bf16[16,128,256]{1,2,0:T(8,128)(2,1)}), bf16[16,128,256]{1,2,0:T(8,128)(2,1)S(1)}, u32[]{:S(2)}, u32[]{:S(2)}) async-start(bf16[16,128,256]{1,2,0:T(8,128)(2,1)} %fusion.3), calls=%async_computation.2 | async-start | bytes 2097152 | tf_op jit(solution)/shard_map/all_to_all | solution.py:83
  294.8 250.1 %all-reduce.6.cloned.1.call-start = ((), (), s32[]{:S(2)}) async-start(), calls=%async_computation.7 | async-start | bytes 524288 | tf_op jit(solution)/shard_map/psum | solution.py:96
  301.7 243.2 %copy-start = (bf16[1,32,4096]{2,1,0:T(8,128)(2,1)S(1)}, bf16[1,32,4096]{2,1,0:T(8,128)(2,1)}, u32[]{:S(2)}) copy-start(bf16[1,32,4096]{2,1,0:T(8,128)(2,1)} %param.7) | copy-start | bytes 786436
  301.7 243.2 %copy-start.2 = (f32[4096]{0:T(1024)S(1)}, f32[4096]{0:T(1024)}, u32[]{:S(2)}) copy-start(f32[4096]{0:T(1024)} %param.8) | copy-start | bytes 49156
Sparse Core Ops, SparseCore 0:
  11.2 155.1 all-reduce.3
  169.1 105.8 all-gather.1
  289.7 103.3 reduce-scatter.1
  395.6 149.2 all-reduce.5
where the time goes:
time: 640 us
  waiting for transfers between devices  439 us (69%)
  blocking collectives  119 us (19%)
  starting transfers between devices  30.4 us (5%)
  matrix products  19.9 us (3%)
  between operations  14.6 us (2%)
  local copies, waits for them, and re-layouts  9.89 us (2%)
  other arithmetic  7.1 us (1%)
    psum x1, waiting for transfers between devices, broadcast(): return lax.psum(block, axis)  156 us
    psum x1, waiting for transfers between devices, on_device(): memory_grad = lax.psum(section_part, 'section').astype(jnp.float32)  150 us
    reduce_scatter x1, waiting for transfers between devices, on_device(): lax.psum_scatter((lax.dot_general(both_grads, w_both, (((1,), (1,)), ((),...  91.4 us
    psum x1, blocking collectives, on_device(): lax.psum(jnp.sum(memory_grad * normed, axis=0) * is_last, ('section', 'dp'))  85.3 us
    unnamed x1, blocking collectives  33.3 us
    all_to_all x1, waiting for transfers between devices, on_device(): lax.all_to_all(queries[0], 'dp', split_axis=1, concat_axis=0, tiled=True)  26.1 us
    all_to_all x1, starting transfers between devices, on_device(): lax.all_to_all(queries[0], 'dp', split_axis=1, concat_axis=0, tiled=True)  19.1 us
    all_gather x1, waiting for transfers between devices, on_device(): lax.all_gather(sent, 'dp', axis=0, tiled=True)  15.6 us
  transfers between devices with their start and end apart: 7, of which 5 were waited for; matrix products, arithmetic and copies ran while one was open for 4% of the time, Pallas kernels for 0%

commit v1 on v0

--- a/solution.py
+++ b/solution.py
@@ -5,6 +5,7 @@
 
 HEAD_DIM = 256
 epsilon = 1e-06
+end_strips_all_up = lambda buf: lax.psum(lax.psum(buf, axis_name="dp"), axis_name="section")
 
 
 def broadcast(block, axis, holder):
@@ -99,7 +100,7 @@
         scaled_grad - normed * jnp.mean(scaled_grad * normed, axis=1, keepdims=True)
     )
     state_grad = (last_grad * is_last).astype(jnp.bfloat16)[None]
-    gain_grad = lax.psum(jnp.sum(memory_grad * normed, axis=0) * is_last, ("section", "dp"))
+    gain_grad = end_strips_all_up(jnp.sum(memory_grad * normed, axis=0) * is_last)
     key_weight_grad = weight_grads[:, :local_width][None]
     value_weight_grad = weight_grads[:, local_width:][None]
     return (query_grad, key_weight_grad, value_weight_grad, state_grad, gain_grad)

time: 640 us -> 726 us (1.13)
  the two profiles are of different devices: /device:TPU:1 before, /device:TPU:0 now
where the time goes in v1:
time: 726 us; the launch traced here: 725 us
  waiting for transfers between devices  457 us (63%)
  blocking collectives  198 us (27%)
  matrix products  20 us (3%)
  starting transfers between devices  19.2 us (3%)
  between operations  14.6 us (2%)
  local copies, waits for them, and re-layouts  9.89 us (1%)
    psum x1, waiting for transfers between devices, broadcast(): return lax.psum(block, axis)  164 us
    psum x1, waiting for transfers between devices, on_device(): memory_grad = lax.psum(section_part, 'section').astype(jnp.float32)  158 us
    reduce_scatter x1, waiting for transfers between devices, on_device(): lax.psum_scatter((lax.dot_general(both_grads, w_both, (((1,), (1,)), ((),...  94 us
    psum x1, blocking collectives, lax.psum(buf, axis_name='dp')  84.2 us
    psum x1, blocking collectives, lax.psum(lax.psum(buf, axis_name='dp'), axis_name='section')  79.1 us
    unnamed x1, blocking collectives  34.6 us
    all_to_all x1, waiting for transfers between devices, on_device(): lax.all_to_all(queries[0], 'dp', split_axis=1, concat_axis=0, tiled=True)  26.5 us
  transfers between devices with their start and end apart: 7, of which 5 were waited for; matrix products, arithmetic and copies ran while one was open for 3% of the time, Pallas kernels for 0%

profile of v1, /device:TPU:0, one launch (start us, length us, event | category | flops | bytes accessed | tf_op | source)
XLA Modules:
  0.0 725.5 jit_solution(6851115538229664736)
XLA Ops:
  7.2 0.0 copy-start.1
  7.2 0.0 all-reduce.4.cloned.1.call-start
  7.2 1.2 fusion.28
  8.4 1.8 fusion.33
  10.2 0.0 all-reduce.4.cloned.1.call-update
  10.3 0.0 all-gather.2.cloned.1.call-start
  10.3 163.6 %all-reduce.4.cloned.1.call-done = bf16[32,4096]{1,0:T(8,128)(2,1)} async-done(((bf16[32,4096]{1,0:T(8,128)(2,1)}), bf16[32,4096]{1,0:T(8,128)(2,1)}) %all-reduce.4.cloned.1.call-update) | async-done | bytes 262160 | tf_op jit(solution)/shard_map/psum | solution.py:13
  173.9 0.0 all-gather.2.cloned.1.call-update
  174.0 1.6 copy.13
  175.6 1.3 copy.14
  176.9 8.4 %all-to-all-start = ((bf16[128,16,256]{2,0,1:T(8,128)(2,1)}), bf16[128,16,256]{2,0,1:T(8,128)(2,1)S(1)}, u32[]{:S(2)}, u32[]{:S(2)}) async-start(bf16[128,16,256]{2,0,1:T(8,128)(2,1)} %copy.14), calls=%async_computation | async-start | bytes 2097152 | tf_op jit(solution)/shard_map/all_to_all | solution.py:42
  185.3 0.0 copy-done.1
  185.3 0.7 copy.15
  186.0 1.3 copy.16
  187.3 26.5 %all-to-all-done = bf16[128,16,256]{2,0,1:T(8,128)(2,1)S(1)} async-done(((bf16[128,16,256]{2,0,1:T(8,128)(2,1)}), bf16[128,16,256]{2,0,1:T(8,128)(2,1)S(1)}, u32[]{:S(2)}, u32[]{:S(2)}) %all-to-all-start) | async-done | bytes 1048608 | tf_op jit(solution)/shard_map/all_to_all | solution.py:42
  213.8 7.0 all-to-all-start.1
  220.9 0.0 reduce-scatter.2.cloned.1.call-start
  221.6 0.0 copy-done.3
  221.6 0.6 dynamic-slice
  222.2 0.8 dynamic-update-slice
  222.9 34.6 %all-reduce = s32[16]{0:T(128)S(1)} all-reduce(s32[16]{0:T(128)S(1)} %dynamic-update-slice), channel_id=1, replica_groups=mesh['section'=16,'dp'=16] {'dp'}, use_global_device_ids=true, to_apply=%add | all-reduce | flops 16 | bytes 128
  257.5 0.1 iota_compare_fusion
  257.6 14.4 %all-gather.2.cloned.1.call-done = bf16[512,4096]{1,0:T(8,128)(2,1)} async-done(((bf16[32,4096]{1,0:T(8,128)(2,1)}), bf16[512,4096]{1,0:T(8,128)(2,1)}) %all-gather.2.cloned.1.call-update) | async-done | bytes 4194320 | tf_op jit(solution)/shard_map/all_gather | solution.py:34
  272.1 5.8 fusion.4
  277.9 0.5 fusion.10
  278.4 0.6 fusion.46
  279.0 0.0 all-to-all-done.1
  279.0 0.5 fusion.13
  279.5 0.3 convolution_convert_fusion.1
  279.8 0.3 convolution_convert_fusion.2
  280.1 6.6 multiply_convert_fusion
  286.7 0.0 reduce-scatter.2.cloned.1.call-update
  286.7 1.5 fusion.3
  288.1 3.7 all-to-all-start.2
  291.8 0.0 all-reduce.6.cloned.1.call-start
  291.9 4.6 multiply_convert_fusion.1
  296.4 2.3 slice_bitcast_fusion
  298.7 94.0 %reduce-scatter.2.cloned.1.call-done = bf16[32,4096]{1,0:T(8,128)(2,1)} async-done(((bf16[512,4096]{1,0:T(8,128)(2,1)}), bf16[32,4096]{1,0:T(8,128)(2,1)}) %reduce-scatter.2.cloned.1.call-update) | async-done | bytes 262160 | tf_op jit(solution)/shard_map/reduce_scatter | solution.py:86
  392.7 0.0 all-reduce.6.cloned.1.call-update
  392.7 0.0 all-to-all-done.2
  392.7 0.3 multiply_convert_fusion.2
  393.0 1.3 copy.17
  394.3 158.1 %all-reduce.6.cloned.1.call-done = bf16[32,4096]{1,0:T(8,128)(2,1)} async-done(((bf16[32,4096]{1,0:T(8,128)(2,1)}), bf16[32,4096]{1,0:T(8,128)(2,1)}) %all-reduce.6.cloned.1.call-update) | async-done | bytes 262160 | tf_op jit(solution)/shard_map/psum | solution.py:97
  552.4 0.0 copy-done
  552.5 1.3 fusion.27
  553.7 84.2 %psum.30 = f32[4096]{0:T(1024)S(1)} all-reduce(f32[4096]{0:T(1024)S(1)} %broadcast_multiply_fusion), channel_id=1, replica_groups=mesh['section'=16,'dp'=16] {'dp'}, use_global_device_ids=true, to_apply=%region_9.10 | all-reduce | flops 4096 | bytes 32768 | tf_op jit(solution)/shard_map/psum | solution.py:8
  637.9 79.1 %psum.31 = f32[4096]{0:T(1024)} all-reduce(f32[4096]{0:T(1024)S(1)} %psum.30), channel_id=1, replica_groups=mesh['section'=16,'dp'=16] {'section'}, use_global_device_ids=true, to_apply=%region_10.11 | all-reduce | flops 4096 | bytes 32768 | tf_op jit(solution)/shard_map/psum | solution.py:8
  717.1 1.8 fusion.34
  (9 shorter events, 0.1 us)
Async XLA Ops:
  7.2 178.1 %copy-start.1 = (bf16[1,128,4096]{2,1,0:T(8,128)(2,1)S(1)}, bf16[1,128,4096]{2,1,0:T(8,128)(2,1)}, u32[]{:S(2)}) copy-start(bf16[1,128,4096]{2,1,0:T(8,128)(2,1)} %param.12) | copy-start | bytes 3145732
  7.2 166.8 %all-reduce.4.cloned.1.call-start = ((), (), s32[]{:S(2)}) async-start(), calls=%async_computation.4 | async-start | bytes 524288 | tf_op jit(solution)/shard_map/psum | solution.py:13
  10.3 261.8 %all-gather.2.cloned.1.call-start = ((), (), s32[]{:S(2)}) async-start(), calls=%async_computation.5 | async-start | bytes 4456448 | tf_op jit(solution)/shard_map/all_gather | solution.py:34
  176.9 44.7 %copy-start.3 = (u32[256]{0:T(256)S(1)}, u32[256]{0:T(256)}, u32[]{:S(2)}) copy-start(u32[256]{0:T(256)} %constant.31) | copy-start | bytes 3076
  176.9 36.9 %all-to-all-start = ((bf16[128,16,256]{2,0,1:T(8,128)(2,1)}), bf16[128,16,256]{2,0,1:T(8,128)(2,1)S(1)}, u32[]{:S(2)}, u32[]{:S(2)}) async-start(bf16[128,16,256]{2,0,1:T(8,128)(2,1)} %copy.14), calls=%async_computation | async-start | bytes 2097152 | tf_op jit(solution)/shard_map/all_to_all | solution.py:42
  213.8 65.2 %all-to-all-start.1 = ((bf16[128,16,256]{2,0,1:T(8,128)(2,1)}), bf16[128,16,256]{2,0,1:T(8,128)(2,1)S(1)}, u32[]{:S(2)}, u32[]{:S(2)}) async-start(bf16[128,16,256]{2,0,1:T(8,128)(2,1)} %copy.16), calls=%async_computation.1 | async-start | bytes 2097152 | tf_op jit(solution)/shard_map/all_to_all | solution.py:43
  220.9 171.9 %reduce-scatter.2.cloned.1.call-start = ((), (), s32[]{:S(2)}) async-start(), calls=%async_computation.6 | async-start | bytes 4456448 | tf_op jit(solution)/shard_map/reduce_scatter | solution.py:86
  288.1 104.6 %all-to-all-start.2 = ((bf16[16,128,256]{1,2,0:T(8,128)(2,1)}), bf16[16,128,256]{1,2,0:T(8,128)(2,1)S(1)}, u32[]{:S(2)}, u32[]{:S(2)}) async-start(bf16[16,128,256]{1,2,0:T(8,128)(2,1)} %fusion.3), calls=%async_computation.2 | async-start | bytes 2097152 | tf_op jit(solution)/shard_map/all_to_all | solution.py:84
  291.8 260.6 %all-reduce.6.cloned.1.call-start = ((), (), s32[]{:S(2)}) async-start(), calls=%async_computation.7 | async-start | bytes 524288 | tf_op jit(solution)/shard_map/psum | solution.py:97
  298.7 253.7 %copy-start = (bf16[1,32,4096]{2,1,0:T(8,128)(2,1)S(1)}, bf16[1,32,4096]{2,1,0:T(8,128)(2,1)}, u32[]{:S(2)}) copy-start(bf16[1,32,4096]{2,1,0:T(8,128)(2,1)} %param.7) | copy-start | bytes 786436
  298.7 253.7 %copy-start.2 = (f32[4096]{0:T(1024)S(1)}, f32[4096]{0:T(1024)}, u32[]{:S(2)}) copy-start(f32[4096]{0:T(1024)} %param.8) | copy-start | bytes 49156
Sparse Core Ops, SparseCore 0:
  11.2 162.7 all-reduce.3
  176.6 95.3 all-gather.1
  286.8 105.8 reduce-scatter.1
  395.2 157.2 all-reduce.5
